TPU v7x, 32 devices: a whole 2x2x4 slice. The times are simulated.
32 devices in a mesh: row: 2 (over core), col: 4 (over y, x), ch: 4 (over z).
Axes of the slice: x: 2, y: 2, z: 4, core: 2. Of those that a mesh axis runs over, the one named last changes fastest.
Arguments:
- grad_out: float32 [4096, 1024], P(('row', 'col'), 'ch'), may hold values from -6 to 6
- relu_mask: int32 [4096, 1024], P(('row', 'col'), 'ch'), may hold values 0 or 1
- saved_agg: float32 [4096, 1024], P(('row', 'col'), 'ch'), may hold values from -0.1875 to 0.1875
- weight: float32 [1024, 1024], P('ch'), may hold values from -0.1875 to 0.1875
- tile_vals: float32 [2, 4, 128, 128, 128], P('row', 'col'), may hold values from -0.125 to 0.125
- tile_pos: int32 [2, 4, 128], P('row', 'col'), may hold values from 0 to 127, as said below
- tile_count: int32 [2, 4], P('row', 'col'), may hold values from 32 to 128, as said below
Outputs:
- weight_grad: float32 [1024, 1024], P(('row', 'col'), 'ch')
- input_grad: float32 [4096, 1024], P('col', 'ch')
Inputs may be any that keep to these rules, and one draw needn't show every extreme that they name: `tile_pos`: each block's entries are a permutation of 0 to 127; the first tile_count of them are the block's nonzero tiles, the others list its zero tiles and their slots' values are ignored. `tile_count`: some block is full in every draw.
All inputs are finite; a program needn't handle non-finite values. No bound on the sum of `relu_mask` on one device may be relied on, other than what follows from the above.
Results may differ from a plain program's by a relative error of at most 0.0003.
Values sent between devices are 32-bit elements; how exact they have to be, the bound alone decides.
A program may use at most 128 MiB of HBM per device.

v0:
```python
import jax
import jax.numpy as jnp
from jax import lax
from jax.sharding import PartitionSpec as P

TILE = 128
OUT_TILES = 16
IN_TILES = 8
HIGHEST = lax.Precision.HIGHEST


def block_grad(tile_set, positions, live_count, grad_rows):
    slot_total = tile_set.shape[0]
    channels = grad_rows.shape[1]
    active = (jnp.arange(slot_total, dtype=jnp.int32) < live_count).astype(jnp.float32)
    out_tile = positions // IN_TILES
    in_tile = positions % IN_TILES
    blocks = grad_rows.reshape(OUT_TILES, TILE, channels)
    picked = jnp.take(blocks, out_tile, axis=0)
    product = jnp.einsum("tij,tif->tjf", tile_set, picked, precision=HIGHEST)
    onehot = (in_tile[:, None] == jnp.arange(IN_TILES, dtype=jnp.int32)[None, :]).astype(
        jnp.float32
    ) * active[:, None]
    summed = jnp.einsum("tc,tjf->cjf", onehot, product, precision=HIGHEST)
    return summed.reshape(IN_TILES * TILE, channels)


def per_device(grad_out, relu_mask, saved_agg, weight, tile_vals, tile_pos, tile_count):
    masked = grad_out * relu_mask.astype(jnp.float32)
    contract_rows = (((0,), (0,)), ((), ()))
    full_masked = lax.all_gather(masked, "ch", axis=1, tiled=True)
    partial_value = lax.dot_general(
        saved_agg, full_masked, contract_rows, precision=HIGHEST, preferred_element_type=jnp.float32
    )
    regrouped = lax.all_to_all(partial_value, "ch", split_axis=1, concat_axis=0, tiled=True)
    weight_grad = lax.psum_scatter(regrouped, ("row", "col"), scatter_dimension=0, tiled=True)
    agg_grad = lax.dot_general(
        full_masked,
        weight,
        (((1,), (1,)), ((), ())),
        precision=HIGHEST,
        preferred_element_type=jnp.float32,
    )
    grad_rows = lax.all_gather(agg_grad, "col", axis=0, tiled=True)
    partial_input = block_grad(tile_vals[0, 0], tile_pos[0, 0], tile_count[0, 0], grad_rows)
    input_grad = lax.psum(partial_input, "row")
    return (weight_grad, input_grad)


def solution(mesh):
    in_specs = (
        P(("row", "col"), "ch"),
        P(("row", "col"), "ch"),
        P(("row", "col"), "ch"),
        P("ch", None),
        P("row", "col", None, None, None),
        P("row", "col", None),
        P("row", "col"),
    )
    out_specs = (P(("row", "col"), "ch"), P("col", "ch"))
    return jax.shard_map(
        per_device, mesh=mesh, in_specs=in_specs, out_specs=out_specs, check_vma=False
    )
```

profile of v0, /device:TPU:0, one launch (start us, length us, event | category | flops | bytes accessed | tf_op | source)
XLA Modules:
  0.0 203.6 jit_solution(18225518108952591362)
XLA Ops:
  7.2 0.0 copy-start
  7.2 0.0 all-gather.3.cloned.1.call-start
  7.2 2.1 %convert_multiply_fusion = f32[512,256]{1,0:T(8,128)} fusion(f32[512,256]{1,0:T(8,128)} %param.7, s32[512,256]{1,0:T(8,128)} %param.8), kind=kLoop, calls=%fused_computation.8 | loop fusion | flops 262144 | bytes 1572864 | tf_op jit(solution)/shard_map/mul | solution.py:29
  9.4 0.0 all-gather.3.cloned.1.call-update
  9.4 0.0 all-gather.5.cloned.1.call-start
  9.4 49.1 %all-gather.3.cloned.1.call-done = f32[512,1024]{1,0:T(8,128)} async-done(((f32[512,256]{1,0:T(8,128)}), f32[512,1024]{1,0:T(8,128)}) %all-gather.3.cloned.1.call-update) | async-done | bytes 2097168 | tf_op jit(solution)/shard_map/all_gather | solution.py:31
  58.5 0.0 copy-done
  58.5 4.2 %fusion.16 = f32[512,256]{1,0:T(8,128)} fusion(f32[512,1024]{1,0:T(8,128)} %all-gather.3.cloned.1.call-done, f32[256,1024]{1,0:T(8,128)S(1)} %copy-done), kind=kOutput, calls=%fused_computation.35 | convolution fusion | flops 1610612736 | bytes 3670016 | tf_op jit(solution)/shard_map/dot_general | solution.py:37
  62.8 0.0 all-gather.5.cloned.1.call-update
  62.8 6.1 %fusion.15 = f32[1024,256]{1,0:T(8,128)} fusion(f32[512,1024]{1,0:T(8,128)} %all-gather.3.cloned.1.call-done, f32[512,256]{1,0:T(8,128)} %param.9), kind=kOutput, calls=%fused_computation.34 | convolution fusion | flops 1610612736 | bytes 3670016 | tf_op jit(solution)/shard_map/dot_general | solution.py:32
  68.9 3.5 %all-to-all-start = ((f32[256,4,256]{0,2,1:T(8,128)}), f32[256,4,256]{0,2,1:T(8,128)S(1)}, u32[]{:S(2)}, u32[]{:S(2)}) async-start(f32[256,4,256]{0,2,1:T(8,128)} %bitcast.1), calls=%async_computation | async-start | bytes 2097152 | tf_op jit(solution)/shard_map/all_to_all | solution.py:35
  72.4 0.0 reduce-scatter.2.cloned.1.call-start
  73.1 0.7 fusion.12
  73.8 0.7 compare_and_fusion
  74.5 0.7 and_select_fusion.2
  75.1 23.1 %all-to-all-done = f32[256,4,256]{0,2,1:T(8,128)S(1)} async-done(((f32[256,4,256]{0,2,1:T(8,128)}), f32[256,4,256]{0,2,1:T(8,128)S(1)}, u32[]{:S(2)}, u32[]{:S(2)}) %all-to-all-start) | async-done | bytes 1048608 | tf_op jit(solution)/shard_map/all_to_all | solution.py:35
  98.2 1.3 copy.10
  99.5 0.0 reduce-scatter.2.cloned.1.call-update
  99.5 0.2 all-reduce.2.cloned.1.call-start
  99.8 0.0 all-gather.5.cloned.1.call-done
  99.8 11.7 %gather_fusion = f32[128,128,256]{2,1,0:T(8,128)} fusion(f32[16,128,256]{2,1,0:T(8,128)} %bitcast.51, s32[1024]{0:T(1024)S(1)} %pad_clamp_fusion), kind=kCustom, calls=%fused_computation | custom fusion | bytes 33554944 | tf_op jit(solution)/shard_map/jit(_take)/gather | solution.py:19
  111.5 34.6 %fusion.2 = f32[128,256,128]{2,1,0:T(8,128)} fusion(f32[128,128,256]{2,1,0:T(8,128)} %gather_fusion, f32[1,1,128,128,128]{4,3,2,1,0:T(8,128)} %param.11, pred[128]{0:T(512)(128)(4,1)S(1)} %compare_and_fusion), kind=kOutput, calls=%fused_computation.3 | convolution fusion | flops 6446645248 | bytes 41943168 | tf_op jit(solution)/shard_map/tij,tif->tjf/dot_general | solution.py:20
  146.1 0.0 copy-start.1
  146.1 17.8 %copy.12 = f32[128,256,128]{1,0,2:T(8,128)} copy(f32[128,256,128]{2,1,0:T(8,128)} %fusion.2) | data formatting | bytes 33554432 | tf_op jit(solution)/shard_map/tij,tif->tjf/dot_general | solution.py:20
  163.8 10.8 %fusion = f32[8,128,256]{2,0,1:T(8,128)S(1)} fusion(f32[128,256,128]{1,0,2:T(8,128)} %copy.12, f32[128]{0:T(128)S(1)} %compare_convert_fusion, s32[128]{0:T(128)S(1)} %and_select_fusion.2), kind=kOutput, calls=%fused_computation.1 | convolution fusion | flops 402655232 | bytes 17826816 | tf_op jit(solution)/shard_map/tc,tjf->cjf/dot_general | solution.py:24
  174.7 1.3 copy.11
  176.0 0.0 all-reduce.2.cloned.1.call-update
  176.0 0.0 reduce-scatter.2.cloned.1.call-done
  176.1 18.7 %all-reduce.2.cloned.1.call-done = f32[1024,256]{1,0:T(8,128)} async-done(((f32[1024,256]{1,0:T(8,128)}), f32[1024,256]{1,0:T(8,128)}) %all-reduce.2.cloned.1.call-update) | async-done | bytes 1048592 | tf_op jit(solution)/shard_map/psum | solution.py:46
  194.8 2.3 %copy.15 = f32[1024,256]{1,0:T(8,128)} copy(f32[1024,256]{1,0:T(8,128)} %all-reduce.2.cloned.1.call-done) | data formatting | bytes 2097152
  197.0 0.0 copy-done.1
  (2 shorter events, 0.0 us)
Async XLA Ops:
  7.2 51.4 %copy-start = (f32[256,1024]{1,0:T(8,128)S(1)}, f32[256,1024]{1,0:T(8,128)}, u32[]{:S(2)}) copy-start(f32[256,1024]{1,0:T(8,128)} %param.10) | copy-start | bytes 3145732
  7.2 51.4 %all-gather.3.cloned.1.call-start = ((), (), s32[]{:S(2)}) async-start(), calls=%async_computation.2 | async-start | bytes 2621440 | tf_op jit(solution)/shard_map/all_gather | solution.py:31
  9.4 90.4 %all-gather.5.cloned.1.call-start = ((), (), s32[]{:S(2)}) async-start(), calls=%async_computation.4 | async-start | bytes 2621440 | tf_op jit(solution)/shard_map/all_gather | solution.py:44
  68.9 29.3 %all-to-all-start = ((f32[256,4,256]{0,2,1:T(8,128)}), f32[256,4,256]{0,2,1:T(8,128)S(1)}, u32[]{:S(2)}, u32[]{:S(2)}) async-start(f32[256,4,256]{0,2,1:T(8,128)} %bitcast.1), calls=%async_computation | async-start | bytes 2097152 | tf_op jit(solution)/shard_map/all_to_all | solution.py:35
  72.4 103.7 %reduce-scatter.2.cloned.1.call-start = ((), (), s32[]{:S(2)}) async-start(), calls=%async_computation.3 | async-start | bytes 1179648 | tf_op jit(solution)/shard_map/reduce_scatter | solution.py:36
  99.5 95.2 %all-reduce.2.cloned.1.call-start = ((), (), s32[]{:S(2)}) async-start(), calls=%async_computation.5 | async-start | bytes 2097152 | tf_op jit(solution)/shard_map/psum | solution.py:46
  146.1 51.0 %copy-start.1 = (f32[256,1024]{1,0:T(8,128)S(1)}, f32[256,1024]{1,0:T(8,128)}, u32[]{:S(2)}) copy-start(f32[256,1024]{1,0:T(8,128)} %param.10) | copy-start | bytes 3145732
Sparse Core Ops, SparseCore 0:
  10.1 48.3 all-gather.2
  62.9 33.9 all-gather.4
  100.7 35.9 reduce-scatter.1
  176.2 18.5 all-reduce.1
where the time goes:
time: 204 us
  waiting for transfers between devices  91 us (45%)
  matrix products  55.7 us (27%)
  local copies, waits for them, and re-layouts  34.4 us (17%)
  between operations  14.5 us (7%)
  other arithmetic  4.15 us (2%)
  starting transfers between devices  3.86 us (2%)
    all_gather x1, waiting for transfers between devices, per_device(): full_masked = lax.all_gather(masked, 'ch', axis=1, tiled=True)  49.1 us
    dot_general x1, matrix products, block_grad(): product = jnp.einsum('tij,tif->tjf', tile_set, picked, precision=HIGHEST)  34.6 us
    all_to_all x1, waiting for transfers between devices, per_device(): lax.all_to_all(partial_value, 'ch', split_axis=1, concat_axis=0, tiled=True)  23.1 us
    psum x1, waiting for transfers between devices, per_device(): input_grad = lax.psum(partial_input, 'row')  18.7 us
    dot_general x1, local copies, waits for them, and re-layouts, block_grad(): product = jnp.einsum('tij,tif->tjf', tile_set, picked, precision=HIGHEST)  17.8 us
    gather x1, local copies, waits for them, and re-layouts, block_grad(): picked = jnp.take(blocks, out_tile, axis=0)  11.7 us
    dot_general x1, matrix products, block_grad(): summed = jnp.einsum('tc,tjf->cjf', onehot, product, precision=HIGHEST)  10.8 us
    dot_general x1, matrix products, per_device(): lax.dot_general(saved_agg, full_masked, contract_rows, precision=HIGHEST,...  6.08 us
  transfers between devices with their start and end apart: 5, of which 3 were waited for; matrix products, arithmetic and copies ran while one was open for 42% of the time, Pallas kernels for 0%

commit v1 on v0

--- a/solution.py
+++ b/solution.py
@@ -43,7 +43,7 @@
     )
     grad_rows = lax.all_gather(agg_grad, "col", axis=0, tiled=True)
     partial_input = block_grad(tile_vals[0, 0], tile_pos[0, 0], tile_count[0, 0], grad_rows)
-    input_grad = lax.psum(partial_input, "row")
+    input_grad = jnp.sum(lax.all_gather(partial_input, "row"), axis=0)
     return (weight_grad, input_grad)
 
 

time: 204 us -> 250 us (1.23)
  blocking collectives: 0 us -> 29.9 us
  waiting for transfers between devices: 91 us -> 112 us
  starting transfers between devices: 3.86 us -> 0.34 us
  other arithmetic: 4.15 us -> 6.97 us
  local copies, waits for them, and re-layouts: 34.4 us -> 31.9 us
    reduce_scatter x1, waiting for transfers between devices: 0.02 us -> 31.4 us  [per_device(): lax.psum_scatter(regrouped, ('row', 'col'), scatter_dimension=0, tiled=True)]
    all_gather x1, waiting for transfers between devices: 0.02 us -> 31.2 us  [per_device(): grad_rows = lax.all_gather(agg_grad, 'col', axis=0, tiled=True)]
    all_to_all x0 -> x1, blocking collectives: none -> 29.9 us  [per_device(): lax.all_to_all(partial_value, 'ch', split_axis=1, concat_axis=0, tiled=True)]
    all_to_all x1 -> x0, waiting for transfers between devices: 23.1 us -> none  [per_device(): lax.all_to_all(partial_value, 'ch', split_axis=1, concat_axis=0, tiled=True)]
    psum x1 -> x0, waiting for transfers between devices: 18.7 us -> none  [per_device(): input_grad = lax.psum(partial_input, 'row')]
    all_to_all x1 -> x0, starting transfers between devices: 3.52 us -> none  [per_device(): lax.all_to_all(partial_value, 'ch', split_axis=1, concat_axis=0, tiled=True)]
    reduce_sum x0 -> x1, other arithmetic: none -> 2.82 us  [per_device(): input_grad = jnp.sum(lax.all_gather(partial_input, 'row'), axis=0)]
  transfers between devices with their start and end apart: 5 -> 4, of which waited for: 3 -> 3; matrix products, arithmetic and copies ran while one was open for 42% -> 4% of each run, Pallas kernels for 0% -> 0%
where the time goes in v1:
time: 250 us
  waiting for transfers between devices  112 us (45%)
  matrix products  54.2 us (22%)
  local copies, waits for them, and re-layouts  31.9 us (13%)
  blocking collectives  29.9 us (12%)
  between operations  14.5 us (6%)
  other arithmetic  6.97 us (3%)
    all_gather x1, waiting for transfers between devices, per_device(): full_masked = lax.all_gather(masked, 'ch', axis=1, tiled=True)  49.1 us
    dot_general x1, matrix products, block_grad(): product = jnp.einsum('tij,tif->tjf', tile_set, picked, precision=HIGHEST)  34.5 us
    reduce_scatter x1, waiting for transfers between devices, per_device(): lax.psum_scatter(regrouped, ('row', 'col'), scatter_dimension=0, tiled=True)  31.4 us
    all_gather x1, waiting for transfers between devices, per_device(): grad_rows = lax.all_gather(agg_grad, 'col', axis=0, tiled=True)  31.2 us
    all_to_all x1, blocking collectives, per_device(): lax.all_to_all(partial_value, 'ch', split_axis=1, concat_axis=0, tiled=True)  29.9 us
    dot_general x1, local copies, waits for them, and re-layouts, block_grad(): product = jnp.einsum('tij,tif->tjf', tile_set, picked, precision=HIGHEST)  17.8 us
    gather x1, local copies, waits for them, and re-layouts, block_grad(): picked = jnp.take(blocks, out_tile, axis=0)  11.4 us
    dot_general x1, matrix products, block_grad(): summed = jnp.einsum('tc,tjf->cjf', onehot, product, precision=HIGHEST)  11 us
  transfers between devices with their start and end apart: 4, of which 3 were waited for; matrix products, arithmetic and copies ran while one was open for 4% of the time, Pallas kernels for 0%

profile of v1, /device:TPU:0, one launch (start us, length us, event | category | flops | bytes accessed | tf_op | source)
XLA Modules:
  0.0 249.6 jit_solution(14934166291815169755)
XLA Ops:
  7.2 0.0 copy-start
  7.2 0.0 all-gather.4.cloned.1.call-start
  7.2 2.1 convert_multiply_fusion
  9.4 0.0 all-gather.4.cloned.1.call-update
  9.4 0.0 all-gather.6.cloned.1.call-start
  9.4 49.1 %all-gather.4.cloned.1.call-done = f32[512,1024]{1,0:T(8,128)} async-done(((f32[512,256]{1,0:T(8,128)}), f32[512,1024]{1,0:T(8,128)}) %all-gather.4.cloned.1.call-update) | async-done | bytes 2097168 | tf_op jit(solution)/shard_map/all_gather | solution.py:31
  58.5 0.0 copy-done
  58.5 4.2 %fusion.18 = f32[512,256]{1,0:T(8,128)} fusion(f32[512,1024]{1,0:T(8,128)} %all-gather.4.cloned.1.call-done, f32[256,1024]{1,0:T(8,128)S(1)} %copy-done), kind=kOutput, calls=%fused_computation.35 | convolution fusion | flops 1610612736 | bytes 3670016 | tf_op jit(solution)/shard_map/dot_general | solution.py:37
  62.8 0.0 all-gather.6.cloned.1.call-update
  62.8 0.2 all-gather.8.cloned.1.call-start
  63.7 0.7 fusion.14
  64.4 0.7 compare_and_fusion
  65.0 0.7 and_select_fusion.2
  65.7 31.2 %all-gather.6.cloned.1.call-done = f32[2048,256]{1,0:T(8,128)} async-done(((f32[512,256]{1,0:T(8,128)}), f32[2048,256]{1,0:T(8,128)}) %all-gather.6.cloned.1.call-update) | async-done | bytes 2097168 | tf_op jit(solution)/shard_map/all_gather | solution.py:44
  96.9 11.4 %gather_fusion = f32[128,128,256]{2,1,0:T(8,128)} fusion(f32[16,128,256]{2,1,0:T(8,128)} %bitcast.51, s32[1024]{0:T(1024)S(1)} %pad_clamp_fusion), kind=kCustom, calls=%fused_computation | custom fusion | bytes 33554944 | tf_op jit(solution)/shard_map/jit(_take)/gather | solution.py:19
  108.4 34.5 %fusion.2 = f32[128,128,256]{1,2,0:T(8,128)} fusion(f32[128,128,256]{2,1,0:T(8,128)} %gather_fusion, f32[1,1,128,128,128]{4,3,2,1,0:T(8,128)} %param.11, pred[128]{0:T(512)(128)(4,1)S(1)} %compare_and_fusion), kind=kOutput, calls=%fused_computation.3 | convolution fusion | flops 6446645248 | bytes 41943168 | tf_op jit(solution)/shard_map/tij,tif->tjf/dot_general | solution.py:20
  142.9 0.0 copy-start.1
  142.9 17.8 %copy.17 = f32[128,128,256]{2,0,1:T(8,128)} copy(f32[128,128,256]{1,2,0:T(8,128)} %fusion.2) | data formatting | bytes 33554432 | tf_op jit(solution)/shard_map/tij,tif->tjf/dot_general | solution.py:20
  160.7 0.0 copy-start.2
  160.7 11.0 %fusion.8 = f32[8,128,256]{2,0,1:T(8,128)S(1)} fusion(f32[128,128,256]{2,0,1:T(8,128)} %copy.17, f32[128]{0:T(128)S(1)} %compare_convert_fusion, s32[128]{0:T(128)S(1)} %and_select_fusion.2), kind=kOutput, calls=%fused_computation.9 | convolution fusion | flops 402655232 | bytes 17826816 | tf_op jit(solution)/shard_map/tc,tjf->cjf/dot_general | solution.py:24
  171.6 1.3 copy.18
  172.9 0.0 all-gather.8.cloned.1.call-update
  173.0 0.0 reduce-scatter.2.cloned.1.call-start
  173.0 0.0 copy-done.2
  173.0 4.5 %fusion.17 = f32[1024,256]{1,0:T(8,128)S(1)} fusion(f32[512,1024]{1,0:T(8,128)S(1)} %copy-done.2, f32[512,256]{1,0:T(8,128)} %param.9), kind=kOutput, calls=%fused_computation.34 | convolution fusion | flops 1610612736 | bytes 3670016 | tf_op jit(solution)/shard_map/dot_general | solution.py:32
  177.5 29.9 %all_to_all.19 = f32[256,4,256]{0,2,1:T(8,128)S(1)} all-to-all(f32[256,4,256]{0,2,1:T(8,128)S(1)} %bitcast.52), channel_id=1, replica_groups=mesh['row'=2,'col'=4,'ch'=4] {'ch'}, dimensions={1} | all-to-all | bytes 2097152 | tf_op jit(solution)/shard_map/all_to_all | solution.py:35
  207.5 1.3 copy.15
  208.8 0.0 reduce-scatter.2.cloned.1.call-update
  208.8 0.0 all-gather.8.cloned.1.call-done
  208.8 2.8 %reduce_sum.9 = f32[1024,256]{1,0:T(8,128)} reduce(f32[2,1024,256]{2,1,0:T(8,128)} %all-gather.8.cloned.1.call-done, f32[]{:T(128)} %constant.39.clone.1), dimensions={0}, to_apply=%region_1.2 | reduce | flops 262144 | bytes 3145732 | tf_op jit(solution)/shard_map/reduce_sum | solution.py:46
  211.7 31.4 %reduce-scatter.2.cloned.1.call-done = f32[128,256]{1,0:T(8,128)} async-done(((f32[1024,256]{1,0:T(8,128)}), f32[128,256]{1,0:T(8,128)}) %reduce-scatter.2.cloned.1.call-update) | async-done | bytes 131088 | tf_op jit(solution)/shard_map/reduce_scatter | solution.py:36
  243.1 0.0 copy-done.1
  (2 shorter events, 0.0 us)
Async XLA Ops:
  7.2 51.4 %copy-start = (f32[256,1024]{1,0:T(8,128)S(1)}, f32[256,1024]{1,0:T(8,128)}, u32[]{:S(2)}) copy-start(f32[256,1024]{1,0:T(8,128)} %param.10) | copy-start | bytes 3145732
  7.2 51.4 %all-gather.4.cloned.1.call-start = ((), (), s32[]{:S(2)}) async-start(), calls=%async_computation.2 | async-start | bytes 2621440 | tf_op jit(solution)/shard_map/all_gather | solution.py:31
  9.4 87.5 %all-gather.6.cloned.1.call-start = ((), (), s32[]{:S(2)}) async-start(), calls=%async_computation.4 | async-start | bytes 2621440 | tf_op jit(solution)/shard_map/all_gather | solution.py:44
  62.8 146.0 %all-gather.8.cloned.1.call-start = ((), (), s32[]{:S(2)}) async-start(), calls=%async_computation.5 | async-start | bytes 3145728 | tf_op jit(solution)/shard_map/all_gather | solution.py:46
  142.9 100.2 %copy-start.1 = (f32[256,1024]{1,0:T(8,128)S(1)}, f32[256,1024]{1,0:T(8,128)}, u32[]{:S(2)}) copy-start(f32[256,1024]{1,0:T(8,128)} %param.10) | copy-start | bytes 3145732
  160.7 12.4 %copy-start.2 = (f32[512,1024]{1,0:T(8,128)S(1)}, f32[512,1024]{1,0:T(8,128)}, u32[]{:S(2)}) copy-start(f32[512,1024]{1,0:T(8,128)} %all-gather.4.cloned.1.call-done) | copy-start | bytes 6291460
  173.0 70.1 %reduce-scatter.2.cloned.1.call-start = ((), (), s32[]{:S(2)}) async-start(), calls=%async_computation.3 | async-start | bytes 1179648 | tf_op jit(solution)/shard_map/reduce_scatter | solution.py:36
Sparse Core Ops, SparseCore 0:
  10.1 48.3 all-gather.3
  62.9 33.9 all-gather.5
  173.1 10.5 all-gather.7
  208.9 34.1 reduce-scatter.1
